TPU v7x, 256 devices: a whole 4x4x8 slice. The times are simulated.
256 devices in a mesh: row: 32 (over z, x_hi, core), col: 8 (over y, x_lo).
Axes of the slice: x: 4 (x_hi: 2, x_lo: 2; x = x_hi * 2 + x_lo), y: 4, z: 8, core: 2. Of those that a mesh axis runs over, the one named last changes fastest.
Arguments:
- s_matrix: bfloat16 [2, 16384, 32768], P(None, 'row', 'col'), may hold values from -0.046875 to 0.046875
- slab: bfloat16 [2, 32768, 384], P(None, ('col', 'row')), may hold values from -6 to 6
- beam_hkl: int32 [3, 32768], P(None, ('col', 'row')), may hold values from -24 to 24
Outputs:
- squared: bfloat16 [2, 16384, 384], P(None, 'row', 'col')
All inputs are finite; a program needn't handle non-finite values.
Results may differ from a plain program's by a relative error of at most 0.014.
Values may be sent and summed in bfloat16 or wider, within the bound.
A program may use at most 64 MiB of HBM per device.

v0:
```python
import jax
import jax.numpy as jnp
from jax import lax
from jax.sharding import PartitionSpec as P


def apply_phase(slab, beam_hkl):
    hkl_float = beam_hkl.astype(jnp.float32)
    angles = (
        0.61
        * (hkl_float[0] * hkl_float[0] + hkl_float[1] * hkl_float[1] + hkl_float[2] * hkl_float[2])
        + 0.29 * hkl_float[0]
        - 0.17 * hkl_float[1]
        + 0.43 * hkl_float[2]
    )
    cosine = jnp.cos(angles)[:, None]
    sine = jnp.sin(angles)[:, None]
    slab_real = slab[0].astype(jnp.float32)
    slab_imag = slab[1].astype(jnp.float32)
    phased_real = cosine * slab_real - sine * slab_imag
    phased_imag = cosine * slab_imag + sine * slab_real
    return jnp.stack([phased_real, phased_imag]).astype(jnp.bfloat16)


def per_device(s_matrix, slab, beam_hkl):
    phased = apply_phase(slab, beam_hkl)
    gathered = lax.all_gather(phased, "row", axis=1, tiled=True)
    s_real = s_matrix[0]
    s_imag = s_matrix[1]
    part_real = jnp.dot(s_real, gathered[0], preferred_element_type=jnp.float32) - jnp.dot(
        s_imag, gathered[1], preferred_element_type=jnp.float32
    )
    part_imag = jnp.dot(s_real, gathered[1], preferred_element_type=jnp.float32) + jnp.dot(
        s_imag, gathered[0], preferred_element_type=jnp.float32
    )
    totals = jnp.stack([part_real, part_imag])
    return lax.psum_scatter(totals.astype(jnp.bfloat16), "col", scatter_dimension=2, tiled=True)


def solution(mesh):
    placed = (P(None, "row", "col"), P(None, ("col", "row"), None), P(None, ("col", "row")))
    return jax.shard_map(
        per_device, mesh=mesh, in_specs=placed, out_specs=P(None, "row", "col"), check_vma=False
    )
```

profile of v0, /device:TPU:4, one launch (start us, length us, event | category | flops | bytes accessed | tf_op | source)
XLA Modules:
  0.0 166.7 jit_solution(7687445948443255985)
XLA Ops:
  6.5 0.0 all-gather.2.cloned.1.call-start
  6.5 0.7 convert_element_type.15
  7.2 0.1 cosine_bitcast_fusion
  7.3 1.1 fusion.31
  8.4 0.7 pad_maximum_fusion.1
  9.1 0.0 all-gather.2.cloned.1.call-update
  9.1 0.0 reduce-scatter.2.cloned.1.call-start
  9.2 95.0 %all-gather.2.cloned.1.call-done = bf16[2,4096,384]{2,1,0:T(8,128)(2,1)} async-done(((bf16[2,128,384]{2,1,0:T(8,128)(2,1)}), bf16[2,4096,384]{2,1,0:T(8,128)(2,1)}) %all-gather.2.cloned.1.call-update) | async-done | bytes 6291472 | tf_op jit(solution)/shard_map/all_gather | solution.py:27
  104.2 0.0 copy-start
  104.2 5.1 %fusion = f32[384,512]{1,0:T(8,128)S(1)} fusion(bf16[2,512,4096]{2,1,0:T(8,128)(2,1)} %param.3, bf16[2,4096,384]{2,1,0:T(8,128)(2,1)} %all-gather.2.cloned.1.call-done), kind=kOutput, calls=%fused_computation | convolution fusion | flops 1610612736 | bytes 8126464 | tf_op jit(solution)/shard_map/dot_general | solution.py:33
  109.3 0.4 copy-done
  109.7 0.0 copy-start.1
  109.7 3.9 %fusion.2 = f32[384,512]{1,0:T(8,128)S(1)} fusion(bf16[2,512,4096]{2,1,0:T(8,128)(2,1)S(1)} %copy-done, bf16[2,4096,384]{2,1,0:T(8,128)(2,1)} %all-gather.2.cloned.1.call-done), kind=kOutput, calls=%fused_computation.2 | convolution fusion | flops 1610612736 | bytes 8126464 | tf_op jit(solution)/shard_map/dot_general | solution.py:30
  113.7 0.0 copy-done.1
  113.7 1.8 %fusion.27 = bf16[1,512,384]{1,2,0:T(8,128)(2,1)S(1)} fusion(f32[384,512]{1,0:T(8,128)S(1)} %fusion, bf16[2,512,4096]{2,1,0:T(8,128)(2,1)S(1)} %copy-done, bf16[2,4096,384]{2,1,0:T(8,128)(2,1)S(1)} %copy-done.1), kind=kOutput, calls=%fused_computation.19 | convolution fusion | flops 1611005952 | bytes 8519680 | tf_op jit(solution)/shard_map/dot_general | solution.py:33
  115.5 1.8 %fusion.24 = bf16[1,512,384]{1,2,0:T(8,128)(2,1)S(1)} fusion(f32[384,512]{1,0:T(8,128)S(1)} %fusion.2, bf16[2,512,4096]{2,1,0:T(8,128)(2,1)S(1)} %copy-done, bf16[2,4096,384]{2,1,0:T(8,128)(2,1)S(1)} %copy-done.1), kind=kOutput, calls=%fused_computation.18 | convolution fusion | flops 1611005952 | bytes 8519680 | tf_op jit(solution)/shard_map/dot_general | solution.py:30
  117.4 1.0 pad_maximum_fusion
  118.3 0.0 reduce-scatter.2.cloned.1.call-update
  118.3 41.5 %reduce-scatter.2.cloned.1.call-done = bf16[2,512,48]{1,2,0:T(8,128)(2,1)} async-done(((bf16[2,512,384]{1,2,0:T(8,128)(2,1)}), bf16[2,512,48]{1,2,0:T(8,128)(2,1)}) %reduce-scatter.2.cloned.1.call-update) | async-done | bytes 98320 | tf_op jit(solution)/shard_map/reduce_scatter | solution.py:37
  (1 shorter events, 0.0 us)
Async XLA Ops:
  6.5 97.7 %all-gather.2.cloned.1.call-start = ((), (), s32[]{:S(2)}) async-start(), calls=%async_computation.1 | async-start | bytes 6488064 | tf_op jit(solution)/shard_map/all_gather | solution.py:27
  9.1 150.7 %reduce-scatter.2.cloned.1.call-start = ((), (), s32[]{:S(2)}) async-start(), calls=%async_computation.2 | async-start | bytes 884736 | tf_op jit(solution)/shard_map/reduce_scatter | solution.py:37
  104.2 5.5 %copy-start = (bf16[2,512,4096]{2,1,0:T(8,128)(2,1)S(1)}, bf16[2,512,4096]{2,1,0:T(8,128)(2,1)}, u32[]{:S(2)}) copy-start(bf16[2,512,4096]{2,1,0:T(8,128)(2,1)} %param.3) | copy-start | bytes 25165828
  109.7 3.9 %copy-start.1 = (bf16[2,4096,384]{2,1,0:T(8,128)(2,1)S(1)}, bf16[2,4096,384]{2,1,0:T(8,128)(2,1)}, u32[]{:S(2)}) copy-start(bf16[2,4096,384]{2,1,0:T(8,128)(2,1)} %all-gather.2.cloned.1.call-done) | copy-start | bytes 18874372
Sparse Core Ops, SparseCore 0:
  10.0 94.1 all-gather.1
  118.5 41.3 reduce-scatter.1
where the time goes:
time: 167 us
  waiting for transfers between devices  137 us (82%)
  between operations  13.5 us (8%)
  matrix products  12.7 us (8%)
  other arithmetic  3.46 us (2%)
    all_gather x1, waiting for transfers between devices, per_device(): gathered = lax.all_gather(phased, 'row', axis=1, tiled=True)  95 us
    reduce_scatter x1, waiting for transfers between devices, per_device(): lax.psum_scatter(totals.astype(jnp.bfloat16), 'col', scatter_dimension=2,...  41.5 us
    dot_general x1, matrix products, per_device(): jnp.dot(s_imag, gathered[0], preferred_element_type=jnp.float32)  5.11 us
    dot_general x1, matrix products, per_device(): jnp.dot(s_imag, gathered[1], preferred_element_type=jnp.float32)  3.93 us
  transfers between devices with their start and end apart: 2, of which 2 were waited for; matrix products, arithmetic and copies ran while one was open for 0% of the time, Pallas kernels for 0%

commit v1 on v0

--- a/solution.py
+++ b/solution.py
@@ -24,7 +24,9 @@
 
 def per_device(s_matrix, slab, beam_hkl):
     phased = apply_phase(slab, beam_hkl)
-    gathered = lax.all_gather(phased, "row", axis=1, tiled=True)
+    gathered = jnp.concatenate(
+        lax.all_to_all(jnp.stack([phased] * lax.axis_size("row")), "row", 0, 0), axis=1
+    )
     s_real = s_matrix[0]
     s_imag = s_matrix[1]
     part_real = jnp.dot(s_real, gathered[0], preferred_element_type=jnp.float32) - jnp.dot(

time: 167 us -> 219 us (1.31)
  blocking collectives: 0 us -> 153 us
  waiting for transfers between devices: 137 us -> 38.7 us
  matrix products: 12.7 us -> 7.33 us
  local copies, waits for them, and re-layouts: 0.44 us -> 3.22 us
    all_to_all x0 -> x1, blocking collectives: none -> 153 us  [per_device(): lax.all_to_all(jnp.stack([phased] * lax.axis_size('row')), 'row', 0, 0)]
    all_gather x1 -> x0, waiting for transfers between devices: 95 us -> none  [per_device(): gathered = lax.all_gather(phased, 'row', axis=1, tiled=True)]
    dot_general x1, matrix products: 5.11 us -> 1.83 us  [per_device(): jnp.dot(s_imag, gathered[0], preferred_element_type=jnp.float32)]
    reduce_scatter x1, waiting for transfers between devices: 41.5 us -> 38.7 us  [per_device(): lax.psum_scatter(totals.astype(jnp.bfloat16), 'col', scatter_dimension=2,...]
  transfers between devices with their start and end apart: 2 -> 1, of which waited for: 2 -> 1; matrix products, arithmetic and copies ran while one was open for 0% -> 0% of each run, Pallas kernels for 0% -> 0%
where the time goes in v1:
time: 219 us; the launch traced here: 218 us
  blocking collectives  153 us (70%)
  waiting for transfers between devices  38.7 us (18%)
  between operations  13.5 us (6%)
  matrix products  7.33 us (3%)
  local copies, waits for them, and re-layouts  3.22 us (1%)
  other arithmetic  2.79 us (1%)
    all_to_all x1, blocking collectives, per_device(): lax.all_to_all(jnp.stack([phased] * lax.axis_size('row')), 'row', 0, 0)  153 us
    reduce_scatter x1, waiting for transfers between devices, per_device(): lax.psum_scatter(totals.astype(jnp.bfloat16), 'col', scatter_dimension=2,...  38.7 us
  transfers between devices with their start and end apart: 1, of which 1 were waited for; matrix products, arithmetic and copies ran while one was open for 0% of the time, Pallas kernels for 0%

profile of v1, /device:TPU:4, one launch (start us, length us, event | category | flops | bytes accessed | tf_op | source)
XLA Modules:
  0.0 218.4 jit_solution(11321501463978996665)
XLA Ops:
  6.5 0.0 reduce-scatter.2.cloned.1.call-start
  6.5 0.7 convert_element_type.17
  7.2 0.1 cosine_bitcast_fusion
  7.3 1.1 fusion.31
  8.4 1.0 stack.14
  9.4 0.0 slice-start
  9.5 152.9 %all_to_all.5 = bf16[32,2,128,384]{3,2,1,0:T(8,128)(2,1)S(1)} all-to-all(bf16[32,2,128,384]{3,2,1,0:T(8,128)(2,1)S(1)} %stack.14), channel_id=1, replica_groups=mesh['row'=32,'col'=8] {'row'}, dimensions={0} | all-to-all | bytes 12582912 | tf_op jit(solution)/shard_map/all_to_all | solution.py:28
  162.4 0.0 slice-start.1
  162.4 1.2 fusion.34
  163.5 0.0 slice-done
  163.5 1.0 slice-done.1
  164.6 1.8 fusion
  166.4 1.8 fusion.2
  168.2 1.8 fusion.27
  170.1 1.8 fusion.24
  171.9 1.0 pad_maximum_fusion
  172.9 0.0 reduce-scatter.2.cloned.1.call-update
  172.9 38.7 %reduce-scatter.2.cloned.1.call-done = bf16[2,512,48]{1,2,0:T(8,128)(2,1)} async-done(((bf16[2,512,384]{1,2,0:T(8,128)(2,1)}), bf16[2,512,48]{1,2,0:T(8,128)(2,1)}) %reduce-scatter.2.cloned.1.call-update) | async-done | bytes 98320 | tf_op jit(solution)/shard_map/reduce_scatter | solution.py:39
  (3 shorter events, 0.1 us)
Async XLA Ops:
  6.5 205.1 %reduce-scatter.2.cloned.1.call-start = ((), (), s32[]{:S(2)}) async-start(), calls=%async_computation.2 | async-start | bytes 884736 | tf_op jit(solution)/shard_map/reduce_scatter | solution.py:39
  9.4 154.1 %slice-start = ((s8[8388608]{0:T(1024)(128)(4,1)}), s8[4194304]{0:T(1024)(128)(4,1)S(1)}, s32[]{:S(2)}) async-start(s8[8388608]{0:T(1024)(128)(4,1)} %bitcast.46), calls=%async_computation.3 | async-start | bytes 8388608
  162.4 2.2 %slice-start.1 = ((s8[8388608]{0:T(1024)(128)(4,1)}), s8[4194304]{0:T(1024)(128)(4,1)S(1)}, s32[]{:S(2)}) async-start(s8[8388608]{0:T(1024)(128)(4,1)} %bitcast.46), calls=%async_computation.4 | async-start | bytes 8388608
Sparse Core Ops, SparseCore 0:
  173.0 38.5 reduce-scatter.1
